TPU v7x, 32 devices: a whole 2x2x4 slice. The times are simulated.
32 devices in a mesh: dp: 8 (over z, y), tensor: 4 (over x, core).
Axes of the slice: x: 2, y: 2, z: 4, core: 2. Of those that a mesh axis runs over, the one named last changes fastest.
Arguments:
- tokens: bfloat16 [16384, 1536], P(('dp', 'tensor')), may hold values from -6 to 6
- segments: int32 [16384], P('dp'), may hold values from 0 to 3, as said below
- positions: int32 [16384], P('dp'), may hold values from 0 to 2044, as said below
- norm_attn: float32 [1536], replicated, may hold values from 0.1 to 1.9
- w_query: bfloat16 [1536, 1536], P(None, 'tensor'), may hold values from -0.15625 to 0.15625
- key_weight: bfloat16 [1536, 768], P(None, 'tensor'), may hold values from -0.15625 to 0.15625
- value_weight: bfloat16 [1536, 768], P(None, 'tensor'), may hold values from -0.15625 to 0.15625
- w_out: bfloat16 [1536, 1536], P('tensor'), may hold values from -1.5 to 1.5
- norm_mlp: float32 [1536], replicated, may hold values from 0.1 to 1.9
- w_gate: bfloat16 [1536, 4096], P(None, 'tensor'), may hold values from -0.15625 to 0.15625
- w_up: bfloat16 [1536, 4096], P(None, 'tensor'), may hold values from -0.15625 to 0.15625
- w_down: bfloat16 [4096, 1536], P('tensor'), may hold values from -0.09375 to 0.09375
- cotangent: bfloat16 [16384, 1536], P(('dp', 'tensor')), may hold values from -6 to 6
Outputs:
- output: bfloat16 [16384, 1536], P(('dp', 'tensor'))
- grad_tokens: float32 [16384, 1536], P(('dp', 'tensor'))
- grad_norm_attn: float32 [1536], replicated
- grad_w_query: float32 [1536, 1536], P(None, 'tensor')
- grad_w_key: float32 [1536, 768], P(None, 'tensor')
- grad_w_value: float32 [1536, 768], P(None, 'tensor')
- grad_w_out: float32 [1536, 1536], P('tensor')
- grad_norm_mlp: float32 [1536], replicated
- grad_w_gate: float32 [1536, 4096], P(None, 'tensor')
- grad_w_up: float32 [1536, 4096], P(None, 'tensor')
- grad_w_down: float32 [4096, 1536], P('tensor')
Inputs may be any that keep to these rules, and one draw needn't show every extreme that they name: `segments`: within each sequence of 2048 tokens the document numbers never fall, start at 0 and end at 3, each document one token or more. `positions`: each token's position within its document, 0 at the document's first token; the first sequence holds a document of 2045 tokens.
All inputs are finite; a program needn't handle non-finite values.
Results may differ from a plain program's by a relative error of at most 0.018.
Values may be sent and summed in bfloat16 or wider, within the bound.
A program may use at most 256 MiB of HBM per device.

v0:
```python
import math
import jax
import jax.numpy as jnp
from jax import lax
from jax.sharding import PartitionSpec as P

HEAD_SIZE = 96
epsilon = 1e-05
rope_base = 100000.0
masked_value = -1e30


def angle_tables(positions, width):
    middle = width // 2
    freq_steps = jnp.arange(middle, dtype=jnp.float32)
    inverse = jnp.exp(freq_steps * (-2.0 * math.log(rope_base) / width))
    angles = positions.astype(jnp.float32)[:, None] * inverse[None, :]
    return (jnp.cos(angles)[:, None, :], jnp.sin(angles)[:, None, :])


def apply_rotary(values, cosine_lookup, sine_lookup):
    middle = values.shape[-1] // 2
    front, second = (values[..., :middle], values[..., middle:])
    return jnp.concatenate(
        [
            front * cosine_lookup - second * sine_lookup,
            second * cosine_lookup + front * sine_lookup,
        ],
        axis=-1,
    )


def rotate_back(grads_in, cosine_lookup, sine_lookup):
    middle = grads_in.shape[-1] // 2
    front, second = (grads_in[..., :middle], grads_in[..., middle:])
    return jnp.concatenate(
        [
            front * cosine_lookup + second * sine_lookup,
            second * cosine_lookup - front * sine_lookup,
        ],
        axis=-1,
    )


def rms_inverse(values):
    return lax.rsqrt(jnp.mean(values * values, axis=-1, keepdims=True) + epsilon)


def norm_back(grad_normed, gain, unit_rows, inverse):
    scaled = grad_normed * gain
    return inverse * (scaled - unit_rows * jnp.mean(scaled * unit_rows, axis=-1, keepdims=True))


def contract_rows(left, right):
    return lax.dot_general(
        left, right, (((0,), (0,)), ((), ())), preferred_element_type=jnp.float32
    )


def contract_cols(left, right):
    return lax.dot_general(
        left, right, (((1,), (1,)), ((), ())), preferred_element_type=jnp.float32
    )


def block_scores(query_block, heads_of_key, allowed, score_scale):
    scores = (
        jnp.einsum("qgrd,kgd->grqk", query_block, heads_of_key, preferred_element_type=jnp.float32)
        * score_scale
    )
    return jnp.where(allowed[None, None], scores, masked_value)


def body(
    tokens,
    segments,
    positions,
    norm_attn,
    w_query,
    key_weight,
    value_weight,
    w_out,
    norm_mlp,
    w_gate,
    w_up,
    w_down,
    cotangent,
):
    sequence_length = segments.shape[0]
    q_heads = w_query.shape[1] // HEAD_SIZE
    kv_heads = key_weight.shape[1] // HEAD_SIZE
    head_repetitions = q_heads // kv_heads
    score_scale = 1.0 / math.sqrt(HEAD_SIZE)
    rows_per_block = min(512, sequence_length)
    block_total = sequence_length // rows_per_block
    cosine_lookup, sine_lookup = angle_tables(positions, HEAD_SIZE)
    indices = jnp.arange(sequence_length, dtype=jnp.int32)
    seg_blocks = segments.reshape(block_total, rows_per_block)
    index_blocks = indices.reshape(block_total, rows_per_block)
    inputs = tokens.astype(jnp.float32)
    inverse_one = rms_inverse(inputs)
    unit_one = inputs * inverse_one
    first_normalized = (unit_one * norm_attn).astype(jnp.bfloat16)
    attn_in = lax.all_gather(first_normalized, "tensor", axis=0, tiled=True)
    query_proj = jnp.dot(attn_in, w_query, preferred_element_type=jnp.float32).reshape(
        sequence_length, q_heads, HEAD_SIZE
    )
    key_proj = jnp.dot(attn_in, key_weight, preferred_element_type=jnp.float32).reshape(
        sequence_length, kv_heads, HEAD_SIZE
    )
    query_rows = apply_rotary(query_proj, cosine_lookup, sine_lookup).astype(jnp.bfloat16)
    heads_of_key = apply_rotary(key_proj, cosine_lookup, sine_lookup).astype(jnp.bfloat16)
    heads_of_value = (
        jnp.dot(attn_in, value_weight, preferred_element_type=jnp.float32)
        .astype(jnp.bfloat16)
        .reshape(sequence_length, kv_heads, HEAD_SIZE)
    )
    blocks_of_query = query_rows.reshape(
        block_total, rows_per_block, kv_heads, head_repetitions, HEAD_SIZE
    )

    def attend(member):
        query_block, rows_seg, rows_idx = member
        allowed = (rows_seg[:, None] == segments[None, :]) & (indices[None, :] <= rows_idx[:, None])
        scores = block_scores(query_block, heads_of_key, allowed, score_scale)
        row_peak = jnp.max(scores, axis=-1, keepdims=True)
        weights = jnp.exp(scores - row_peak)
        totals = jnp.sum(weights, axis=-1, keepdims=True)
        weights_low = (weights / totals).astype(jnp.bfloat16)
        mixed_heads = jnp.einsum(
            "grqk,kgd->qgrd", weights_low, heads_of_value, preferred_element_type=jnp.float32
        )
        return (mixed_heads.astype(jnp.bfloat16), row_peak[..., 0] + jnp.log(totals[..., 0]))

    attended, log_totals = lax.map(attend, (blocks_of_query, seg_blocks, index_blocks))
    attended = attended.reshape(sequence_length, q_heads * HEAD_SIZE)
    row_slice = attended
    attn_out = lax.psum_scatter(
        jnp.dot(row_slice, w_out, preferred_element_type=jnp.float32),
        "tensor",
        scatter_dimension=0,
        tiled=True,
    )
    hidden_one = inputs + attn_out
    inverse_two = rms_inverse(hidden_one)
    unit_two = hidden_one * inverse_two
    normed_two = (unit_two * norm_mlp).astype(jnp.bfloat16)
    mlp_in = lax.all_gather(normed_two, "tensor", axis=0, tiled=True)
    gate_proj = jnp.dot(mlp_in, w_gate, preferred_element_type=jnp.float32)
    up_proj = jnp.dot(mlp_in, w_up, preferred_element_type=jnp.float32)
    sigmoid_gate = jax.nn.sigmoid(gate_proj)
    activated = gate_proj * sigmoid_gate
    hidden = (activated * up_proj).astype(jnp.bfloat16)
    row_slice = hidden
    mlp_out = lax.psum_scatter(
        jnp.dot(row_slice, w_down, preferred_element_type=jnp.float32).astype(jnp.bfloat16),
        "tensor",
        scatter_dimension=0,
        tiled=True,
    ).astype(jnp.float32)
    output = (hidden_one + mlp_out).astype(jnp.bfloat16)
    grad_out = lax.all_gather(cotangent, "tensor", axis=0, tiled=True)
    grad_w_down = contract_rows(hidden, grad_out)
    grad_hidden = contract_cols(grad_out, w_down)
    grad_gate = (
        grad_hidden * up_proj * sigmoid_gate * (1.0 + gate_proj * (1.0 - sigmoid_gate))
    ).astype(jnp.bfloat16)
    grad_upper = (grad_hidden * activated).astype(jnp.bfloat16)
    grad_w_gate = contract_rows(mlp_in, grad_gate)
    grad_w_up = contract_rows(mlp_in, grad_upper)
    grad_normed_two = lax.psum_scatter(
        contract_cols(grad_gate, w_gate) + contract_cols(grad_upper, w_up),
        "tensor",
        scatter_dimension=0,
        tiled=True,
    )
    grad_norm_mlp = jnp.sum(grad_normed_two * unit_two, axis=0)
    grad_hidden_one = cotangent.astype(jnp.float32) + norm_back(
        grad_normed_two, norm_mlp, unit_two, inverse_two
    )
    grad_attn_rows = lax.all_gather(
        grad_hidden_one.astype(jnp.bfloat16), "tensor", axis=0, tiled=True
    )
    grad_w_out = contract_rows(attended, grad_attn_rows)
    grad_attended = contract_cols(grad_attn_rows, w_out).astype(jnp.bfloat16)
    grad_blocks = grad_attended.reshape(
        block_total, rows_per_block, kv_heads, head_repetitions, HEAD_SIZE
    )

    def attend_back(running, member):
        query_block, grad_block, rows_seg, rows_idx, log_block = member
        allowed = (rows_seg[:, None] == segments[None, :]) & (indices[None, :] <= rows_idx[:, None])
        scores = block_scores(query_block, heads_of_key, allowed, score_scale)
        weights = jnp.exp(scores - log_block[..., None])
        grad_weights = jnp.einsum(
            "qgrd,kgd->grqk", grad_block, heads_of_value, preferred_element_type=jnp.float32
        )
        inner_sum = jnp.sum(weights * grad_weights, axis=-1, keepdims=True)
        grad_scores = (weights * (grad_weights - inner_sum)).astype(jnp.bfloat16)
        grad_query = (
            jnp.einsum(
                "grqk,kgd->qgrd", grad_scores, heads_of_key, preferred_element_type=jnp.float32
            )
            * score_scale
        )
        grad_keys = (
            running[0]
            + jnp.einsum(
                "grqk,qgrd->kgd", grad_scores, query_block, preferred_element_type=jnp.float32
            )
            * score_scale
        )
        grad_values = running[1] + jnp.einsum(
            "grqk,qgrd->kgd",
            weights.astype(jnp.bfloat16),
            grad_block,
            preferred_element_type=jnp.float32,
        )
        return ((grad_keys, grad_values), grad_query)

    zero_state = jnp.zeros((sequence_length, kv_heads, HEAD_SIZE), jnp.float32)
    (grad_keys, grad_values), grad_queries = lax.scan(
        attend_back,
        (zero_state, zero_state),
        (blocks_of_query, grad_blocks, seg_blocks, index_blocks, log_totals),
    )
    grad_queries = grad_queries.reshape(sequence_length, q_heads, HEAD_SIZE)
    grad_q_proj = (
        rotate_back(grad_queries, cosine_lookup, sine_lookup)
        .reshape(sequence_length, q_heads * HEAD_SIZE)
        .astype(jnp.bfloat16)
    )
    grad_k_proj = (
        rotate_back(grad_keys, cosine_lookup, sine_lookup)
        .reshape(sequence_length, kv_heads * HEAD_SIZE)
        .astype(jnp.bfloat16)
    )
    grad_v_proj = grad_values.reshape(sequence_length, kv_heads * HEAD_SIZE).astype(jnp.bfloat16)
    grad_w_query = contract_rows(attn_in, grad_q_proj)
    grad_w_key = contract_rows(attn_in, grad_k_proj)
    grad_w_value = contract_rows(attn_in, grad_v_proj)
    grad_normed_one = lax.psum_scatter(
        (
            contract_cols(grad_q_proj, w_query)
            + contract_cols(grad_k_proj, key_weight)
            + contract_cols(grad_v_proj, value_weight)
        ).astype(jnp.bfloat16),
        "tensor",
        scatter_dimension=0,
        tiled=True,
    ).astype(jnp.float32)
    grad_norm_attn = jnp.sum(grad_normed_one * unit_one, axis=0)
    grad_tokens = grad_hidden_one + norm_back(grad_normed_one, norm_attn, unit_one, inverse_one)
    grad_norm_attn, grad_norm_mlp = lax.psum((grad_norm_attn, grad_norm_mlp), ("dp", "tensor"))
    grad_w_query, grad_w_key, grad_w_value, grad_w_out, grad_w_gate, grad_w_up, grad_w_down = (
        lax.psum(grad_w_query.astype(jnp.bfloat16), "dp").astype(jnp.float32),
        lax.psum(grad_w_key.astype(jnp.bfloat16), "dp").astype(jnp.float32),
        lax.psum(grad_w_value.astype(jnp.bfloat16), "dp").astype(jnp.float32),
        lax.psum(grad_w_out.astype(jnp.bfloat16), "dp").astype(jnp.float32),
        lax.psum(grad_w_gate.astype(jnp.bfloat16), "dp").astype(jnp.float32),
        lax.psum(grad_w_up.astype(jnp.bfloat16), "dp").astype(jnp.float32),
        lax.psum(grad_w_down.astype(jnp.bfloat16), "dp").astype(jnp.float32),
    )
    return (
        output,
        grad_tokens,
        grad_norm_attn,
        grad_w_query,
        grad_w_key,
        grad_w_value,
        grad_w_out,
        grad_norm_mlp,
        grad_w_gate,
        grad_w_up,
        grad_w_down,
    )


def solution(mesh):
    in_specs = (
        P(("dp", "tensor"), None),
        P("dp"),
        P("dp"),
        P(),
        P(None, "tensor"),
        P(None, "tensor"),
        P(None, "tensor"),
        P("tensor", None),
        P(),
        P(None, "tensor"),
        P(None, "tensor"),
        P("tensor", None),
        P(("dp", "tensor"), None),
    )
    out_specs = (
        P(("dp", "tensor"), None),
        P(("dp", "tensor"), None),
        P(),
        P(None, "tensor"),
        P(None, "tensor"),
        P(None, "tensor"),
        P("tensor", None),
        P(),
        P(None, "tensor"),
        P(None, "tensor"),
        P("tensor", None),
    )
    return jax.shard_map(body, mesh=mesh, in_specs=in_specs, out_specs=out_specs, check_vma=False)
```

profile of v0, /device:TPU:0, one launch (start us, length us, event | category | flops | bytes accessed | tf_op | source)
XLA Modules:
  0.0 1461.6 jit_solution(5925052065785356915)
XLA Ops:
  15.7 46.3 %all-gather.5.cloned.1.call-done = bf16[2048,1536]{1,0:T(8,128)(2,1)} async-done(((bf16[512,1536]{1,0:T(8,128)(2,1)}), bf16[2048,1536]{1,0:T(8,128)(2,1)}) %all-gather.5.cloned.1.call-update) | async-done | bytes 6291472 | tf_op jit(solution)/shard_map/all_gather | solution.py:104
  62.0 5.2 fusion.71
  84.0 5.9 convolution_convert_fusion.9
  89.8 66.6 %while.28 = (s32[]{:T(128)}, bf16[4,512,2,2,96]{1,4,3,2,0:T(8,128)(2,1)}, f32[4,2,2,512]{3,2,1,0:T(2,128)}, s32[4,512]{1,0:T(4,128)S(1)}, s32[2048]{0:T(1024)S(1...) while((s32[]{:T(128)}, ...), condition=%wide.region_4.5_spmd.clone, body=%wide.region_1.4_spmd.clone.sunk | while | flops 1664284672 | bytes 60117144 | solution.py:135
  91.2 4.7 bitcast_reduce_fusion.2
  96.0 4.4 fusion.143
  100.4 5.6 fusion.144
  107.8 4.7 bitcast_reduce_fusion.2
  112.6 4.4 fusion.143
  117.0 5.6 fusion.144
  124.4 4.7 bitcast_reduce_fusion.2
  129.2 4.4 fusion.143
  133.5 5.6 fusion.144
  141.0 4.7 bitcast_reduce_fusion.2
  145.7 4.4 fusion.143
  150.1 5.6 fusion.144
  160.8 6.4 fusion.72
  167.2 99.1 %reduce-scatter.5.cloned.1.call-done = f32[512,1536]{1,0:T(8,128)} async-done(((f32[2048,1536]{1,0:T(8,128)}), f32[512,1536]{1,0:T(8,128)}) %reduce-scatter.5.cloned.1.call-update) | async-done | bytes 3145744 | tf_op jit(solution)/shard_map/reduce_scatter | solution.py:138
  273.0 45.9 %all-gather.7.cloned.1.call-done = bf16[2048,1536]{1,0:T(8,128)(2,1)} async-done(((bf16[512,1536]{1,0:T(8,128)(2,1)}), bf16[2048,1536]{1,0:T(8,128)(2,1)}) %all-gather.7.cloned.1.call-update) | async-done | bytes 6291472 | tf_op jit(solution)/shard_map/all_gather | solution.py:148
  318.9 12.6 fusion.74
  331.5 8.8 fusion.73
  340.3 26.4 %all-gather.9.cloned.1.call-done = bf16[2048,1536]{1,0:T(8,128)(2,1)} async-done(((bf16[512,1536]{1,0:T(8,128)(2,1)}), bf16[2048,1536]{1,0:T(8,128)(2,1)}) %all-gather.9.cloned.1.call-update) | async-done | bytes 6291472 | tf_op jit(solution)/shard_map/all_gather | solution.py:162
  366.8 18.8 %multiply_convert_fusion = (bf16[2048,1024]{1,0:T(8,128)(2,1)}, bf16[2048,1024]{1,0:T(8,128)(2,1)}, bf16[2048,1024]{1,0:T(8,128)(2,1)}) fusion(f32[2048,1024]{1,0:T(8,128)} %fusion.73, f32[2048,1024]{1,0:T(8,128)} %fusion.74, bf16[2048,1536]{1,0:T(8,128)(2,1)} %all-gather.9.cloned.1.call-done, bf16[1024,1536]{1,0:T(8,128)(2,1)S(1)} %copy-done), kind=kOutput, calls=%fused_computation.69 | convolution fusion | flops 6473908224 | bytes 38797312 | tf_op jit(solution)/shard_map/dot_general | solution.py:61
  385.6 11.6 fusion.75
  397.2 12.9 convolution_add_fusion
  410.1 99.1 %reduce-scatter.9.cloned.1.call-done = f32[512,1536]{1,0:T(8,128)} async-done(((f32[2048,1536]{1,0:T(8,128)}), f32[512,1536]{1,0:T(8,128)}) %reduce-scatter.9.cloned.1.call-update) | async-done | bytes 3145744 | tf_op jit(solution)/shard_map/reduce_scatter | solution.py:171
  517.6 46.5 %all-gather.11.cloned.1.call-done = bf16[2048,1536]{1,0:T(8,128)(2,1)} async-done(((bf16[512,1536]{1,0:T(8,128)(2,1)}), bf16[2048,1536]{1,0:T(8,128)(2,1)}) %all-gather.11.cloned.1.call-update) | async-done | bytes 6291472 | tf_op jit(solution)/shard_map/all_gather | solution.py:181
  564.1 7.7 convolution_convert_fusion.6
  571.8 7.0 reshape.300
  578.7 6.0 copy.29
  584.7 274.0 %while.29 = (s32[]{:T(128)}, f32[2048,2,96]{0,2,1:T(8,128)}, f32[2048,2,96]{0,2,1:T(8,128)}, f32[4,512,2,2,96]{1,0,4,3,2:T(4,128)}, bf16[4,512,2,2,96]{1,4,3,2,0...) while((s32[]{:T(128)}, f32[2048,2,96]{0,2,1:T(8,128)}, ...), condition=%wide.region_12.13_spmd.clone, body=%wide.region_10.12_spmd.clone.sunk | while | flops 4094752768 | bytes 214511840 | solution.py:222
  590.7 5.8 copy-done.1
  596.5 7.1 fusion.158
  603.6 12.6 fusion.155
  616.3 12.2 fusion.156
  636.6 16.1 %dynamic_update_slice.22 = f32[4,512,2,2,96]{1,0,4,3,2:T(4,128)} dynamic-update-slice(f32[4,512,2,2,96]{1,0,4,3,2:T(4,128)} %get-tuple-element.503, f32[1,512,2,2,96]{1,0,4,3,2:T(1,128)} %copy.49, s32[]{:T(128)S(6)} %copy.66, s32[]{:T(128)} %constant.58.clone.1..sunk, s32[]{:T(128)} %constant.58.clone.1..sunk, s32[]{:T(128)} %constant.58.clone.1..sunk, s32[]{:T(128)} %constant.58.clone.1..sunk) | dynamic-update-slice | bytes 1572868 | tf_op jit(solution)/shard_map/while/body/jit(dynamic_update_index_in_dim)/dynamic_update_slice | solution.py:222
  658.2 5.8 copy-done.1
  664.0 7.7 fusion.158
  671.7 12.6 fusion.155
  684.3 12.2 fusion.156
  705.2 16.1 %dynamic_update_slice.22 = f32[4,512,2,2,96]{1,0,4,3,2:T(4,128)} dynamic-update-slice(f32[4,512,2,2,96]{1,0,4,3,2:T(4,128)} %get-tuple-element.503, f32[1,512,2,2,96]{1,0,4,3,2:T(1,128)} %copy.49, s32[]{:T(128)S(6)} %copy.66, s32[]{:T(128)} %constant.58.clone.1..sunk, s32[]{:T(128)} %constant.58.clone.1..sunk, s32[]{:T(128)} %constant.58.clone.1..sunk, s32[]{:T(128)} %constant.58.clone.1..sunk) | dynamic-update-slice | bytes 1572868 | tf_op jit(solution)/shard_map/while/body/jit(dynamic_update_index_in_dim)/dynamic_update_slice | solution.py:222
  726.9 5.8 copy-done.1
  732.7 7.7 fusion.158
  740.3 12.6 fusion.155
  753.0 12.2 fusion.156
  773.8 16.1 %dynamic_update_slice.22 = f32[4,512,2,2,96]{1,0,4,3,2:T(4,128)} dynamic-update-slice(f32[4,512,2,2,96]{1,0,4,3,2:T(4,128)} %get-tuple-element.503, f32[1,512,2,2,96]{1,0,4,3,2:T(1,128)} %copy.49, s32[]{:T(128)S(6)} %copy.66, s32[]{:T(128)} %constant.58.clone.1..sunk, s32[]{:T(128)} %constant.58.clone.1..sunk, s32[]{:T(128)} %constant.58.clone.1..sunk, s32[]{:T(128)} %constant.58.clone.1..sunk) | dynamic-update-slice | bytes 1572868 | tf_op jit(solution)/shard_map/while/body/jit(dynamic_update_index_in_dim)/dynamic_update_slice | solution.py:222
  795.5 5.8 copy-done.1
  801.3 7.7 fusion.158
  809.0 12.6 fusion.155
  821.6 12.2 fusion.156
  842.5 16.1 %dynamic_update_slice.22 = f32[4,512,2,2,96]{1,0,4,3,2:T(4,128)} dynamic-update-slice(f32[4,512,2,2,96]{1,0,4,3,2:T(4,128)} %get-tuple-element.503, f32[1,512,2,2,96]{1,0,4,3,2:T(1,128)} %copy.49, s32[]{:T(128)S(6)} %copy.66, s32[]{:T(128)} %constant.58.clone.1..sunk, s32[]{:T(128)} %constant.58.clone.1..sunk, s32[]{:T(128)} %constant.58.clone.1..sunk, s32[]{:T(128)} %constant.58.clone.1..sunk) | dynamic-update-slice | bytes 1572868 | tf_op jit(solution)/shard_map/while/body/jit(dynamic_update_index_in_dim)/dynamic_update_slice | solution.py:222
  858.7 5.3 reshape.293
  870.0 6.5 fusion.76
  876.6 6.4 fusion.77
  883.0 12.8 add_convert_fusion
  895.9 10.9 convolution_convert_fusion
  906.9 12.0 convolution_convert_fusion.2
  919.0 10.1 convolution_convert_fusion.3
  929.1 8.5 convolution_convert_fusion.1
  945.8 4.5 convolution_convert_fusion.5
  957.3 40.1 %all-reduce = (f32[1536]{0:T(1024)}, f32[1536]{0:T(1024)}) all-reduce(f32[1536]{0:T(1024)S(1)} %get-tuple-element.234, f32[1536]{0:T(1024)S(1)} %copy-done.41), channel_id=1, replica_groups=mesh['dp'=8,'tensor'=4] {'dp','tensor'}, use_global_device_ids=true, to_apply=%region_16.17 | all-reduce | flops 3072 | bytes 24576 | tf_op jit(solution)/shard_map/psum | solution.py:254
  997.4 19.3 %reduce-scatter.7.cloned.1.call-done = bf16[512,1536]{1,0:T(8,128)(2,1)} async-done(((bf16[2048,1536]{1,0:T(8,128)(2,1)}), bf16[512,1536]{1,0:T(8,128)(2,1)}) %reduce-scatter.7.cloned.1.call-update) | async-done | bytes 1572880 | tf_op jit(solution)/shard_map/reduce_scatter | solution.py:155
  1016.7 7.0 fusion.64
  1023.7 413.4 %all-reduce.4.cloned.1.call-done = (bf16[1536,384]{1,0:T(8,128)(2,1)}, bf16[1536,192]{0,1:T(8,128)(2,1)}, bf16[1536,192]{0,1:T(8,128)(2,1)}, bf16[384,1536]{1,0:...) async-done(((bf16[1536,384]{1,0:T(8,128)(2,1)}, bf16[1536,192]{0,1:T(8,128)(2,1)}, bf16[1536,192]{0,1:T(8,128)(2,1)}, ...) | async-done | bytes 12976144 | tf_op jit(solution)/shard_map/psum | solution.py:256
  (244 shorter events, 146.7 us)
Async XLA Ops:
  7.2 359.6 %copy-start = (bf16[1024,1536]{1,0:T(8,128)(2,1)S(1)}, bf16[1024,1536]{1,0:T(8,128)(2,1)}, u32[]{:S(2)}) copy-start(bf16[1024,1536]{1,0:T(8,128)(2,1)} %param.28) | copy-start | bytes 9437188
  7.2 5.7 copy-start.29
  7.2 5.7 copy-start.46
  7.2 54.8 %all-gather.5.cloned.1.call-start = ((), (), s32[]{:S(2)}) async-start(), calls=%async_computation.4 | async-start | bytes 7864320 | tf_op jit(solution)/shard_map/all_gather | solution.py:104
  12.8 253.6 %reduce-scatter.5.cloned.1.call-start = ((), (), s32[]{:S(2)}) async-start(), calls=%async_computation.5 | async-start | bytes 15728640 | tf_op jit(solution)/shard_map/reduce_scatter | solution.py:138
  15.7 55.7 %copy-start.7 = (f32[2048,48]{0,1:T(8,128)}, f32[2048,48]{0,1:T(8,128)S(1)}, u32[]{:S(2)}) copy-start(f32[2048,48]{0,1:T(8,128)S(1)} %get-tuple-element.310) | copy-start | bytes 1179652
  62.0 5.2 copy-start.9
  62.0 6.4 copy-start.47
  79.1 4.0 copy-start.23
  79.1 4.0 copy-start.24
  84.0 5.9 copy-start.37
  96.0 4.4 copy-start.6
  112.5 4.4 copy-start.6
  129.1 4.4 copy-start.6
  145.7 4.4 copy-start.6
  156.4 4.4 copy-start.26
  167.2 103.7 %copy-start.35 = (f32[1536]{0:T(1024)S(1)}, f32[1536]{0:T(1024)}, u32[]{:S(2)}) copy-start(f32[1536]{0:T(1024)} %param.25) | copy-start | bytes 18436
  167.2 151.7 %all-gather.7.cloned.1.call-start = ((), (), s32[]{:S(2)}) async-start(), calls=%async_computation.6 | async-start | bytes 7864320 | tf_op jit(solution)/shard_map/all_gather | solution.py:148
  269.2 244.4 %copy-start.39 = (f32[512]{0:T(512)}, f32[512]{0:T(512)S(1)}, u32[]{:S(2)}) copy-start(f32[512]{0:T(512)S(1)} %add_rsqrt_fusion) | copy-start | bytes 6148
  272.4 94.4 %all-gather.9.cloned.1.call-start = ((), (), s32[]{:S(2)}) async-start(), calls=%async_computation.8 | async-start | bytes 7864320 | tf_op jit(solution)/shard_map/all_gather | solution.py:162
  273.0 236.3 %reduce-scatter.9.cloned.1.call-start = ((), (), s32[]{:S(2)}) async-start(), calls=%async_computation.9 | async-start | bytes 15728640 | tf_op jit(solution)/shard_map/reduce_scatter | solution.py:171
  318.9 12.6 copy-start.48
  318.9 12.6 copy-start.49
  366.8 18.8 %copy-start.50 = (bf16[1536,1024]{1,0:T(8,128)(2,1)S(1)}, bf16[1536,1024]{1,0:T(8,128)(2,1)}, u32[]{:S(2)}) copy-start(bf16[1536,1024]{1,0:T(8,128)(2,1)} %param.26) | copy-start | bytes 9437188
  385.5 11.6 copy-start.51
  385.5 11.6 copy-start.53
  410.1 154.0 %all-gather.11.cloned.1.call-start = ((), (), s32[]{:S(2)}) async-start(), calls=%async_computation.10 | async-start | bytes 7864320 | tf_op jit(solution)/shard_map/all_gather | solution.py:181
  509.3 4.4 copy-start.4
  509.3 4.7 copy-start.5
  517.5 436.8 %reduce-scatter.11.cloned.1.call-start = ((), (), s32[]{:S(2)}) async-start(), calls=%async_computation.11 | async-start | bytes 7864320 | tf_op jit(solution)/shard_map/reduce_scatter | solution.py:242
  590.7 5.8 copy-start.1
  616.2 12.2 copy-start.2
  658.2 5.8 copy-start.1
  684.3 12.2 copy-start.2
  726.9 5.8 copy-start.1
  753.0 12.2 copy-start.2
  795.5 5.8 copy-start.1
  821.6 12.2 copy-start.2
  858.7 5.3 copy-start.8
  864.0 4.2 copy-start.22
  868.4 14.7 %copy-start.20 = (bf16[2048,2,96]{0,2,1:T(8,128)(2,1)}, bf16[2048,2,96]{0,2,1:T(8,128)(2,1)S(1)}, u32[]{:S(2)}) copy-start(bf16[2048,2,96]{0,2,1:T(8,128)(2,1)S(1)} %convert_element_type.138) | copy-start | bytes 2359300
  868.5 8.0 copy-start.13
  870.0 6.6 copy-start.32
  876.6 6.4 copy-start.15
  876.6 6.4 copy-start.34
  895.8 120.9 %reduce-scatter.7.cloned.1.call-start = ((), (), s32[]{:S(2)}) async-start(), calls=%async_computation.7 | async-start | bytes 7864320 | tf_op jit(solution)/shard_map/reduce_scatter | solution.py:155
  906.8 530.3 %all-reduce.4.cloned.1.call-start = ((), (), s32[]{:S(2)}) async-start(), calls=%async_computation.12 | async-start | bytes 25952256 | tf_op jit(solution)/shard_map/psum | solution.py:256
  906.9 12.1 copy-start.52
  906.9 22.2 %slice-start.2 = ((s8[6291456]{0:T(1024)(128)(4,1)}), s8[4194304]{0:T(1024)(128)(4,1)S(1)}, s32[]{:S(2)}) async-start(s8[6291456]{0:T(1024)(128)(4,1)} %bitcast.262), calls=%async_computation.15 | async-start | bytes 8388608
  918.9 10.2 slice-start.3
  918.9 10.2 copy-start.54
  918.9 18.7 %slice-start = ((s8[6291456]{0:T(1024)(128)(4,1)}), s8[4194304]{0:T(1024)(128)(4,1)S(1)}, s32[]{:S(2)}) async-start(s8[6291456]{0:T(1024)(128)(4,1)} %bitcast.260), calls=%async_computation.13 | async-start | bytes 8388608
  929.1 8.6 copy-start.16
  929.1 8.6 slice-start.1
  937.7 4.4 slice-start.4
  950.3 4.0 copy-start.38
  950.3 4.0 copy-start.43
  950.4 6.9 copy-start.41
  950.4 66.3 %copy-start.36 = (f32[1536]{0:T(1024)S(1)}, f32[1536]{0:T(1024)}, u32[]{:S(2)}) copy-start(f32[1536]{0:T(1024)} %param.25) | copy-start | bytes 18436
  950.4 66.3 %copy-start.40 = (f32[512]{0:T(512)S(1)}, f32[512]{0:T(512)}, u32[]{:S(2)}) copy-start(f32[512]{0:T(512)} %copy-done.39) | copy-start | bytes 6148
  950.4 66.3 %copy-start.45 = (f32[512]{0:T(512)S(1)}, f32[512]{0:T(512)}, u32[]{:S(2)}) copy-start(f32[512]{0:T(512)} %copy-done.44) | copy-start | bytes 6148
  1437.1 4.1 copy-start.30
  1437.1 5.3 copy-start.25
  1440.1 4.0 copy-start.19
  (15 other events, 35.5 us)
Sparse Core Ops, SparseCore 0:
  12.9 49.0 all-gather.4
  167.3 99.0 reduce-scatter.4
  272.5 46.3 all-gather.6
  320.3 46.3 all-gather.8
  410.2 99.0 reduce-scatter.8
  517.7 46.3 all-gather.10
  895.9 58.3 reduce-scatter.10
  957.6 59.0 reduce-scatter.6
  1023.5 413.5 all-reduce.3
where the time goes:
time: 1470 us; the launch traced here: 1460 us
  waiting for transfers between devices  801 us (54%)
  matrix products  336 us (23%)
  other arithmetic  136 us (9%)
  local copies, waits for them, and re-layouts  132 us (9%)
  blocking collectives  40.1 us (3%)
  between operations  14.9 us (1%)
    psum x1, waiting for transfers between devices, body(): lax.psum(grad_w_query.astype(jnp.bfloat16), 'dp').astype(jnp.float32)  413 us
    reduce_scatter x1, waiting for transfers between devices, body(): lax.psum_scatter(contract_cols(grad_gate, w_gate) + contract_cols(grad_up...  99.1 us
    reduce_scatter x1, waiting for transfers between devices, body(): lax.psum_scatter(jnp.dot(row_slice, w_out, preferred_element_type=jnp.flo...  99.1 us
    dot_general x7, matrix products, contract_cols(): lax.dot_general(left, right, (((1,), (1,)), ((), ())), preferred_element_...  76.6 us
    dynamic_update_slice x8, local copies, waits for them, and re-layouts, body(): lax.scan(attend_back, (zero_state, zero_state), (blocks_of_query, grad_bl...  71.2 us
    dot_general x4, matrix products, attend_back(): jnp.einsum('qgrd,kgd->grqk', grad_block, heads_of_value, preferred_elemen...  50.6 us
    convert_element_type x4, other arithmetic, attend_back(): grad_scores = (weights * (grad_weights - inner_sum)).astype(jnp.bfloat16)  48.7 us
    all_gather x1, waiting for transfers between devices, body(): lax.all_gather(grad_hidden_one.astype(jnp.bfloat16), 'tensor', axis=0, ti...  46.5 us
  transfers between devices with their start and end apart: 9, of which 9 were waited for; matrix products, arithmetic and copies ran while one was open for 6% of the time, Pallas kernels for 0%

commit v1 on v0

--- a/solution.py
+++ b/solution.py
@@ -3,6 +3,7 @@
 import jax.numpy as jnp
 from jax import lax
 from jax.sharding import PartitionSpec as P
+from jax.lax import axis_index, axis_size, ppermute
 
 HEAD_SIZE = 96
 epsilon = 1e-05
@@ -145,7 +146,24 @@
     inverse_two = rms_inverse(hidden_one)
     unit_two = hidden_one * inverse_two
     normed_two = (unit_two * norm_mlp).astype(jnp.bfloat16)
-    mlp_in = lax.all_gather(normed_two, "tensor", axis=0, tiled=True)
+    u_next = axis_size("tensor")
+    current_block = axis_index("tensor")
+    new, near, arr_out = (u_next, current_block, normed_two.shape[0])
+    found_now = jnp.zeros(
+        [j0 * new if k == 0 else j0 for k, j0 in enumerate(normed_two.shape)], normed_two.dtype
+    )
+    mlp_in = lax.dynamic_update_slice_in_dim(found_now, normed_two, near * arr_out, axis=0)
+    frame_out = block_next = normed_two
+    for b in tuple(range(1, new // 2 + 1)):
+        frame_out = ppermute(frame_out, "tensor", [(k, (k + 1) % new) for k in range(new)])
+        mlp_in = lax.dynamic_update_slice_in_dim(
+            mlp_in, frame_out, (near - b) % new * arr_out, axis=0
+        )
+        if 2 * b < new:
+            block_next = ppermute(block_next, "tensor", [(k, (k - 1) % new) for k in range(new)])
+            mlp_in = lax.dynamic_update_slice_in_dim(
+                mlp_in, block_next, (near + b) % new * arr_out, axis=0
+            )
     gate_proj = jnp.dot(mlp_in, w_gate, preferred_element_type=jnp.float32)
     up_proj = jnp.dot(mlp_in, w_up, preferred_element_type=jnp.float32)
     sigmoid_gate = jax.nn.sigmoid(gate_proj)

time: 1470 us -> 1450 us (0.986)
  local copies, waits for them, and re-layouts: 132 us -> 115 us
    ppermute x0 -> x3, waiting for transfers between devices: none -> 67.5 us  [the longest x2 67.5 us: body(): ppermute(frame_out, 'tensor', [(k, (k + 1) % new) for k in range(new)])]
    all_gather x1 -> x0, waiting for transfers between devices: 45.9 us -> none  [body(): mlp_in = lax.all_gather(normed_two, 'tensor', axis=0, tiled=True)]
    while x24 -> x64, local copies, waits for them, and re-layouts: 23.2 us -> 0.16 us
    all_gather x1, waiting for transfers between devices: 26.4 us -> 3.56 us  [body(): grad_out = lax.all_gather(cotangent, 'tensor', axis=0, tiled=True)]
  transfers between devices with their start and end apart: 9 -> 11, of which waited for: 9 -> 9; matrix products, arithmetic and copies ran while one was open for 6% -> 6% of each run, Pallas kernels for 0% -> 0%
where the time goes in v1:
time: 1450 us; the launch traced here: 1440 us
  waiting for transfers between devices  799 us (55%)
  matrix products  338 us (23%)
  other arithmetic  130 us (9%)
  local copies, waits for them, and re-layouts  115 us (8%)
  blocking collectives  40 us (3%)
  between operations  15 us (1%)
    psum x1, waiting for transfers between devices, body(): lax.psum(grad_w_query.astype(jnp.bfloat16), 'dp').astype(jnp.float32)  414 us
    reduce_scatter x1, waiting for transfers between devices, body(): lax.psum_scatter(contract_cols(grad_gate, w_gate) + contract_cols(grad_up...  98.7 us
    reduce_scatter x1, waiting for transfers between devices, body(): lax.psum_scatter(jnp.dot(row_slice, w_out, preferred_element_type=jnp.flo...  98.4 us
    ppermute x2, waiting for transfers between devices, body(): ppermute(frame_out, 'tensor', [(k, (k + 1) % new) for k in range(new)])  67.5 us
    dynamic_update_slice x8, local copies, waits for them, and re-layouts, body(): lax.scan(attend_back, (zero_state, zero_state), (blocks_of_query, grad_bl...  67.5 us
    dot_general x7, matrix products, contract_cols(): lax.dot_general(left, right, (((1,), (1,)), ((), ())), preferred_element_...  66.9 us
    all_gather x1, waiting for transfers between devices, body(): lax.all_gather(grad_hidden_one.astype(jnp.bfloat16), 'tensor', axis=0, ti...  46.5 us
    all_gather x1, waiting for transfers between devices, body(): attn_in = lax.all_gather(first_normalized, 'tensor', axis=0, tiled=True)  46.3 us
  transfers between devices with their start and end apart: 11, of which 9 were waited for; matrix products, arithmetic and copies ran while one was open for 6% of the time, Pallas kernels for 0%

profile of v1, /device:TPU:0, one launch (start us, length us, event | category | flops | bytes accessed | tf_op | source)
XLA Modules:
  0.0 1440.3 jit_solution(12531182972081298498)
XLA Ops:
  15.2 46.3 %all-gather.4.cloned.1.call-done = bf16[2048,1536]{1,0:T(8,128)(2,1)} async-done(((bf16[512,1536]{1,0:T(8,128)(2,1)}), bf16[2048,1536]{1,0:T(8,128)(2,1)}) %all-gather.4.cloned.1.call-update) | async-done | bytes 6291472 | tf_op jit(solution)/shard_map/all_gather | solution.py:105
  61.5 5.2 fusion.71
  83.4 5.8 convolution_convert_fusion.9
  89.2 69.3 %while.28 = (s32[]{:T(128)}, bf16[4,512,2,2,96]{1,4,3,2,0:T(8,128)(2,1)}, f32[4,2,2,512]{3,2,1,0:T(2,128)}, s32[4,512]{1,0:T(4,128)S(1)}, s32[2048]{0:T(1024)S(1...) while((s32[]{:T(128)}, ...), condition=%wide.region_4.5_spmd.clone, body=%wide.region_1.4_spmd.clone.sunk | while | flops 1664284672 | bytes 60117144 | solution.py:136
  91.3 4.7 bitcast_reduce_fusion.2
  96.0 4.4 fusion.143
  100.4 5.6 fusion.144
  108.6 4.7 bitcast_reduce_fusion.2
  113.3 4.4 fusion.143
  117.7 5.6 fusion.144
  125.9 4.7 bitcast_reduce_fusion.2
  130.6 4.4 fusion.143
  135.0 5.6 fusion.144
  143.1 4.7 bitcast_reduce_fusion.2
  147.9 4.4 fusion.143
  152.3 5.6 fusion.144
  162.9 6.4 fusion.72
  170.1 98.4 %reduce-scatter.5.cloned.1.call-done = f32[512,1536]{1,0:T(8,128)} async-done(((f32[2048,1536]{1,0:T(8,128)}), f32[512,1536]{1,0:T(8,128)}) %reduce-scatter.5.cloned.1.call-update) | async-done | bytes 3145744 | tf_op jit(solution)/shard_map/reduce_scatter | solution.py:139
  279.0 67.5 %collective-permute-done = bf16[512,1536]{1,0:T(8,128)(2,1)} collective-permute-done((bf16[512,1536]{1,0:T(8,128)(2,1)}, bf16[512,1536]{1,0:T(8,128)(2,1)}, u32[]{:S(2)}, u32[]{:S(2)}) %collective-permute-start) | collective-permute-done | bytes 1572896 | tf_op jit(solution)/shard_map/ppermute | solution.py:158
  350.1 12.6 fusion.74
  370.8 11.3 fusion.73
  382.1 16.4 %multiply_convert_fusion = (bf16[2048,1024]{1,0:T(8,128)(2,1)}, bf16[2048,1024]{1,0:T(8,128)(2,1)}, bf16[2048,1024]{1,0:T(8,128)(2,1)}) fusion(f32[2048,1024]{1,0:T(8,128)} %fusion.74, f32[2048,1024]{1,0:T(8,128)} %fusion.73, bf16[2048,1536]{1,0:T(8,128)(2,1)S(1)} %copy-done.17, bf16[1536,1024]{1,0:T(8,128)(2,1)S(1)} %copy-done), kind=kOutput, calls=%fused_computation.69 | convolution fusion | flops 6473908224 | bytes 38797312 | tf_op jit(solution)/shard_map/dot_general | solution.py:167
  398.5 8.7 fusion.75
  407.2 12.3 convolution_add_fusion
  419.6 98.7 %reduce-scatter.9.cloned.1.call-done = f32[512,1536]{1,0:T(8,128)} async-done(((f32[2048,1536]{1,0:T(8,128)}), f32[512,1536]{1,0:T(8,128)}) %reduce-scatter.9.cloned.1.call-update) | async-done | bytes 3145744 | tf_op jit(solution)/shard_map/reduce_scatter | solution.py:189
  523.9 46.5 %all-gather.8.cloned.1.call-done = bf16[2048,1536]{1,0:T(8,128)(2,1)} async-done(((bf16[512,1536]{1,0:T(8,128)(2,1)}), bf16[2048,1536]{1,0:T(8,128)(2,1)}) %all-gather.8.cloned.1.call-update) | async-done | bytes 6291472 | tf_op jit(solution)/shard_map/all_gather | solution.py:199
  570.3 7.7 convolution_convert_fusion.6
  578.0 6.3 reshape.300
  584.3 4.4 copy.29
  588.7 252.2 %while.29 = (s32[]{:T(128)}, f32[2048,2,96]{0,2,1:T(8,128)}, f32[2048,2,96]{0,2,1:T(8,128)}, f32[4,512,2,2,96]{1,0,4,3,2:T(4,128)}, bf16[4,512,2,2,96]{1,4,3,2,0...) while((s32[]{:T(128)}, f32[2048,2,96]{0,2,1:T(8,128)}, ...), condition=%wide.region_12.13_spmd.clone, body=%wide.region_10.12_spmd.clone.sunk | while | flops 4094752768 | bytes 190525824 | solution.py:240
  595.9 7.2 fusion.158
  603.1 11.3 fusion.155
  614.4 10.9 fusion.156
  625.4 6.4 fusion.159
  635.4 16.1 %dynamic_update_slice.42 = f32[4,512,2,2,96]{1,0,4,3,2:T(4,128)} dynamic-update-slice(f32[4,512,2,2,96]{1,0,4,3,2:T(4,128)} %get-tuple-element.505, f32[1,512,2,2,96]{1,0,4,3,2:T(1,128)S(1)} %copy.49, s32[]{:T(128)S(6)} %copy.70, s32[]{:T(128)} %constant.86.clone.1..sunk, s32[]{:T(128)} %constant.86.clone.1..sunk, s32[]{:T(128)} %constant.86.clone.1..sunk, s32[]{:T(128)} %constant.86.clone.1..sunk) | dynamic-update-slice | bytes 1572868 | tf_op jit(solution)/shard_map/while/body/jit(dynamic_update_index_in_dim)/dynamic_update_slice | solution.py:240
  658.4 7.7 fusion.158
  666.2 11.3 fusion.155
  677.5 10.9 fusion.156
  688.5 6.4 fusion.159
  698.5 16.1 %dynamic_update_slice.42 = f32[4,512,2,2,96]{1,0,4,3,2:T(4,128)} dynamic-update-slice(f32[4,512,2,2,96]{1,0,4,3,2:T(4,128)} %get-tuple-element.505, f32[1,512,2,2,96]{1,0,4,3,2:T(1,128)S(1)} %copy.49, s32[]{:T(128)S(6)} %copy.70, s32[]{:T(128)} %constant.86.clone.1..sunk, s32[]{:T(128)} %constant.86.clone.1..sunk, s32[]{:T(128)} %constant.86.clone.1..sunk, s32[]{:T(128)} %constant.86.clone.1..sunk) | dynamic-update-slice | bytes 1572868 | tf_op jit(solution)/shard_map/while/body/jit(dynamic_update_index_in_dim)/dynamic_update_slice | solution.py:240
  721.5 7.7 fusion.158
  729.3 11.3 fusion.155
  740.6 10.9 fusion.156
  751.6 6.4 fusion.159
  761.6 16.1 %dynamic_update_slice.42 = f32[4,512,2,2,96]{1,0,4,3,2:T(4,128)} dynamic-update-slice(f32[4,512,2,2,96]{1,0,4,3,2:T(4,128)} %get-tuple-element.505, f32[1,512,2,2,96]{1,0,4,3,2:T(1,128)S(1)} %copy.49, s32[]{:T(128)S(6)} %copy.70, s32[]{:T(128)} %constant.86.clone.1..sunk, s32[]{:T(128)} %constant.86.clone.1..sunk, s32[]{:T(128)} %constant.86.clone.1..sunk, s32[]{:T(128)} %constant.86.clone.1..sunk) | dynamic-update-slice | bytes 1572868 | tf_op jit(solution)/shard_map/while/body/jit(dynamic_update_index_in_dim)/dynamic_update_slice | solution.py:240
  784.6 7.7 fusion.158
  792.4 11.3 fusion.155
  803.7 10.9 fusion.156
  814.7 6.4 fusion.159
  824.7 16.1 %dynamic_update_slice.42 = f32[4,512,2,2,96]{1,0,4,3,2:T(4,128)} dynamic-update-slice(f32[4,512,2,2,96]{1,0,4,3,2:T(4,128)} %get-tuple-element.505, f32[1,512,2,2,96]{1,0,4,3,2:T(1,128)S(1)} %copy.49, s32[]{:T(128)S(6)} %copy.70, s32[]{:T(128)} %constant.86.clone.1..sunk, s32[]{:T(128)} %constant.86.clone.1..sunk, s32[]{:T(128)} %constant.86.clone.1..sunk, s32[]{:T(128)} %constant.86.clone.1..sunk) | dynamic-update-slice | bytes 1572868 | tf_op jit(solution)/shard_map/while/body/jit(dynamic_update_index_in_dim)/dynamic_update_slice | solution.py:240
  841.0 4.0 reshape.293
  848.7 6.5 fusion.76
  855.3 6.4 fusion.77
  861.7 12.7 add_convert_fusion
  874.5 11.2 convolution_convert_fusion
  885.8 12.3 convolution_convert_fusion.2
  898.1 10.2 convolution_convert_fusion.3
  908.3 8.4 convolution_convert_fusion.1
  921.2 3.6 convolution_convert_fusion.4
  924.8 4.5 convolution_convert_fusion.5
  935.9 40.0 %all-reduce = (f32[1536]{0:T(1024)}, f32[1536]{0:T(1024)}) all-reduce(f32[1536]{0:T(1024)S(1)} %get-tuple-element.234, f32[1536]{0:T(1024)S(1)} %copy-done.44), channel_id=1, replica_groups=mesh['dp'=8,'tensor'=4] {'dp','tensor'}, use_global_device_ids=true, to_apply=%region_16.17 | all-reduce | flops 3072 | bytes 24576 | tf_op jit(solution)/shard_map/psum | solution.py:272
  975.9 19.4 %reduce-scatter.7.cloned.1.call-done = bf16[512,1536]{1,0:T(8,128)(2,1)} async-done(((bf16[2048,1536]{1,0:T(8,128)(2,1)}), bf16[512,1536]{1,0:T(8,128)(2,1)}) %reduce-scatter.7.cloned.1.call-update) | async-done | bytes 1572880 | tf_op jit(solution)/shard_map/reduce_scatter | solution.py:173
  995.3 6.1 fusion.64
  1001.4 414.3 %all-reduce.4.cloned.1.call-done = (bf16[1536,384]{1,0:T(8,128)(2,1)}, bf16[1536,192]{0,1:T(8,128)(2,1)}, bf16[1536,192]{0,1:T(8,128)(2,1)}, bf16[384,1536]{1,0:...) async-done(((bf16[1536,384]{1,0:T(8,128)(2,1)}, bf16[1536,192]{0,1:T(8,128)(2,1)}, bf16[1536,192]{0,1:T(8,128)(2,1)}, ...) | async-done | bytes 12976144 | tf_op jit(solution)/shard_map/psum | solution.py:274
  (281 shorter events, 141.7 us)
Async XLA Ops:
  7.2 375.0 %copy-start = (bf16[1536,1024]{1,0:T(8,128)(2,1)S(1)}, bf16[1536,1024]{1,0:T(8,128)(2,1)}, u32[]{:S(2)}) copy-start(bf16[1536,1024]{1,0:T(8,128)(2,1)} %param.26) | copy-start | bytes 9437188
  7.2 5.1 copy-start.29
  7.2 5.1 copy-start.49
  7.2 54.2 %all-gather.4.cloned.1.call-start = ((), (), s32[]{:S(2)}) async-start(), calls=%async_computation.4 | async-start | bytes 7864320 | tf_op jit(solution)/shard_map/all_gather | solution.py:105
  12.2 256.3 %reduce-scatter.5.cloned.1.call-start = ((), (), s32[]{:S(2)}) async-start(), calls=%async_computation.5 | async-start | bytes 15728640 | tf_op jit(solution)/shard_map/reduce_scatter | solution.py:139
  15.2 55.7 %copy-start.12 = (f32[2048,48]{0,1:T(8,128)}, f32[2048,48]{0,1:T(8,128)S(1)}, u32[]{:S(2)}) copy-start(f32[2048,48]{0,1:T(8,128)S(1)} %get-tuple-element.312) | copy-start | bytes 1179652
  61.5 5.2 copy-start.14
  61.5 6.4 copy-start.50
  96.0 4.4 copy-start.10
  113.3 4.4 copy-start.10
  130.6 4.4 copy-start.10
  147.9 4.4 copy-start.10
  158.5 4.3 copy-start.26
  169.3 180.8 %all-gather.6.cloned.1.call-start = ((), (), s32[]{:S(2)}) async-start(), calls=%async_computation.7 | async-start | bytes 7864320 | tf_op jit(solution)/shard_map/all_gather | solution.py:180
  170.0 348.2 %reduce-scatter.9.cloned.1.call-start = ((), (), s32[]{:S(2)}) async-start(), calls=%async_computation.8 | async-start | bytes 15728640 | tf_op jit(solution)/shard_map/reduce_scatter | solution.py:189
  271.3 250.3 %copy-start.42 = (f32[512]{0:T(512)}, f32[512]{0:T(512)S(1)}, u32[]{:S(2)}) copy-start(f32[512]{0:T(512)S(1)} %add_rsqrt_fusion) | copy-start | bytes 6148
  277.3 69.3 %collective-permute-start = (bf16[512,1536]{1,0:T(8,128)(2,1)}, bf16[512,1536]{1,0:T(8,128)(2,1)}, u32[]{:S(2)}, u32[]{:S(2)}) collective-permute-start(bf16[512,1536]{1,0:T(8,128)(2,1)} %get-tuple-element.288), channel_id=1, source_target_pairs={{0,1},{1,2},{2,3},{3,0},{4,5},{5,6},{6,7},{7,4},{8,9},{9,10},{10,1... | collective-permute-start | bytes 4718600 | tf_op jit(solution)/shard_map/ppermute | solution.py:158
  277.3 88.1 %collective-permute-start.1 = (bf16[512,1536]{1,0:T(8,128)(2,1)}, bf16[512,1536]{1,0:T(8,128)(2,1)}, u32[]{:S(2)}, u32[]{:S(2)}) collective-permute-start(bf16[512,1536]{1,0:T(8,128)(2,1)} %get-tuple-element.288), channel_id=1, source_target_pairs={{0,3},{1,0},{2,1},{3,2},{4,7},{5,4},{6,5},{7,6},{8,11},{9,8},{10,9... | collective-permute-start | bytes 4718600 | tf_op jit(solution)/shard_map/ppermute | solution.py:163
  346.6 21.6 %collective-permute-start.2 = (bf16[512,1536]{1,0:T(8,128)(2,1)}, bf16[512,1536]{1,0:T(8,128)(2,1)}, u32[]{:S(2)}, u32[]{:S(2)}) collective-permute-start(bf16[512,1536]{1,0:T(8,128)(2,1)} %collective-permute-done), channel_id=1, source_target_pairs={{0,1},{1,2},{2,3},{3,0},{4,5},{5,6},{6,7},{7,4},{8,9},{9,10},{10,1... | collective-permute-start | bytes 4718600 | tf_op jit(solution)/shard_map/ppermute | solution.py:158
  365.3 5.5 copy-start.51
  370.8 11.3 copy-start.17
  398.5 8.7 copy-start.52
  419.5 98.8 %copy-start.7 = (f32[512,1536]{1,0:T(8,128)S(1)}, f32[512,1536]{1,0:T(8,128)}, u32[]{:S(2)}) copy-start(f32[512,1536]{1,0:T(8,128)} %copy-done.6) | copy-start | bytes 9437188
  419.5 150.8 %all-gather.8.cloned.1.call-start = ((), (), s32[]{:S(2)}) async-start(), calls=%async_computation.9 | async-start | bytes 7864320 | tf_op jit(solution)/shard_map/all_gather | solution.py:199
  523.8 409.1 %reduce-scatter.11.cloned.1.call-start = ((), (), s32[]{:S(2)}) async-start(), calls=%async_computation.10 | async-start | bytes 7864320 | tf_op jit(solution)/shard_map/reduce_scatter | solution.py:260
  625.4 6.4 copy-start.2
  625.4 6.4 copy-start.3
  634.5 16.9 %copy-start.4 = (f32[2048,2,96]{0,2,1:T(8,128)}, f32[2048,2,96]{0,2,1:T(8,128)S(1)}, u32[]{:S(2)}) copy-start(f32[2048,2,96]{0,2,1:T(8,128)S(1)} %fusion.157) | copy-start | bytes 4718596 | tf_op jit(solution)/shard_map/while
  634.5 16.9 %copy-start.31 = (s32[2048]{0:T(1024)S(1)}, s32[2048]{0:T(1024)}, u32[]{:S(2)}) copy-start(s32[2048]{0:T(1024)} %copy-done.30) | copy-start | bytes 24580 | tf_op jit(solution)/shard_map/while
  634.5 16.9 %copy-start.40 = (s32[4,512]{1,0:T(4,128)S(1)}, s32[4,512]{1,0:T(4,128)}, u32[]{:S(2)}) copy-start(s32[4,512]{1,0:T(4,128)} %copy-done.39) | copy-start | bytes 24580 | tf_op jit(solution)/shard_map/while
  688.5 6.4 copy-start.2
  688.5 6.4 copy-start.3
  697.6 16.9 %copy-start.4 = (f32[2048,2,96]{0,2,1:T(8,128)}, f32[2048,2,96]{0,2,1:T(8,128)S(1)}, u32[]{:S(2)}) copy-start(f32[2048,2,96]{0,2,1:T(8,128)S(1)} %fusion.157) | copy-start | bytes 4718596 | tf_op jit(solution)/shard_map/while
  697.6 16.9 %copy-start.31 = (s32[2048]{0:T(1024)S(1)}, s32[2048]{0:T(1024)}, u32[]{:S(2)}) copy-start(s32[2048]{0:T(1024)} %copy-done.30) | copy-start | bytes 24580 | tf_op jit(solution)/shard_map/while
  697.6 16.9 %copy-start.40 = (s32[4,512]{1,0:T(4,128)S(1)}, s32[4,512]{1,0:T(4,128)}, u32[]{:S(2)}) copy-start(s32[4,512]{1,0:T(4,128)} %copy-done.39) | copy-start | bytes 24580 | tf_op jit(solution)/shard_map/while
  751.6 6.4 copy-start.2
  751.6 6.4 copy-start.3
  760.7 16.9 %copy-start.4 = (f32[2048,2,96]{0,2,1:T(8,128)}, f32[2048,2,96]{0,2,1:T(8,128)S(1)}, u32[]{:S(2)}) copy-start(f32[2048,2,96]{0,2,1:T(8,128)S(1)} %fusion.157) | copy-start | bytes 4718596 | tf_op jit(solution)/shard_map/while
  760.7 16.9 %copy-start.31 = (s32[2048]{0:T(1024)S(1)}, s32[2048]{0:T(1024)}, u32[]{:S(2)}) copy-start(s32[2048]{0:T(1024)} %copy-done.30) | copy-start | bytes 24580 | tf_op jit(solution)/shard_map/while
  760.7 16.9 %copy-start.40 = (s32[4,512]{1,0:T(4,128)S(1)}, s32[4,512]{1,0:T(4,128)}, u32[]{:S(2)}) copy-start(s32[4,512]{1,0:T(4,128)} %copy-done.39) | copy-start | bytes 24580 | tf_op jit(solution)/shard_map/while
  814.7 6.4 copy-start.2
  814.7 6.4 copy-start.3
  823.8 16.9 %copy-start.4 = (f32[2048,2,96]{0,2,1:T(8,128)}, f32[2048,2,96]{0,2,1:T(8,128)S(1)}, u32[]{:S(2)}) copy-start(f32[2048,2,96]{0,2,1:T(8,128)S(1)} %fusion.157) | copy-start | bytes 4718596 | tf_op jit(solution)/shard_map/while
  823.8 16.9 %copy-start.31 = (s32[2048]{0:T(1024)S(1)}, s32[2048]{0:T(1024)}, u32[]{:S(2)}) copy-start(s32[2048]{0:T(1024)} %copy-done.30) | copy-start | bytes 24580 | tf_op jit(solution)/shard_map/while
  823.8 16.9 %copy-start.40 = (s32[4,512]{1,0:T(4,128)S(1)}, s32[4,512]{1,0:T(4,128)}, u32[]{:S(2)}) copy-start(s32[4,512]{1,0:T(4,128)} %copy-done.39) | copy-start | bytes 24580 | tf_op jit(solution)/shard_map/while
  848.6 6.6 copy-start.34
  855.3 6.4 copy-start.36
  874.4 120.9 %reduce-scatter.7.cloned.1.call-start = ((), (), s32[]{:S(2)}) async-start(), calls=%async_computation.6 | async-start | bytes 7864320 | tf_op jit(solution)/shard_map/reduce_scatter | solution.py:173
  885.8 530.0 %all-reduce.4.cloned.1.call-start = ((), (), s32[]{:S(2)}) async-start(), calls=%async_computation.11 | async-start | bytes 25952256 | tf_op jit(solution)/shard_map/psum | solution.py:274
  885.8 12.3 copy-start.53
  885.8 22.5 %slice-start.2 = ((s8[6291456]{0:T(1024)(128)(4,1)}), s8[4194304]{0:T(1024)(128)(4,1)S(1)}, s32[]{:S(2)}) async-start(s8[6291456]{0:T(1024)(128)(4,1)} %bitcast.262), calls=%async_computation.14 | async-start | bytes 8388608
  898.1 10.2 slice-start.3
  898.1 10.2 copy-start.54
  898.1 18.6 %slice-start = ((s8[6291456]{0:T(1024)(128)(4,1)}), s8[4194304]{0:T(1024)(128)(4,1)S(1)}, s32[]{:S(2)}) async-start(s8[6291456]{0:T(1024)(128)(4,1)} %bitcast.260), calls=%async_computation.12 | async-start | bytes 8388608
  908.3 8.5 slice-start.1
  916.8 4.4 slice-start.4
  929.4 6.5 copy-start.44
  929.4 65.9 %copy-start.8 = (f32[512,1536]{1,0:T(8,128)S(1)}, f32[512,1536]{1,0:T(8,128)}, u32[]{:S(2)}) copy-start(f32[512,1536]{1,0:T(8,128)} %copy-done.6) | copy-start | bytes 9437188
  929.4 65.9 %copy-start.38 = (f32[1536]{0:T(1024)S(1)}, f32[1536]{0:T(1024)}, u32[]{:S(2)}) copy-start(f32[1536]{0:T(1024)} %param.25) | copy-start | bytes 18436
  929.4 65.9 %copy-start.43 = (f32[512]{0:T(512)S(1)}, f32[512]{0:T(512)}, u32[]{:S(2)}) copy-start(f32[512]{0:T(512)} %copy-done.42) | copy-start | bytes 6148
  929.4 65.9 %copy-start.48 = (f32[512]{0:T(512)S(1)}, f32[512]{0:T(512)}, u32[]{:S(2)}) copy-start(f32[512]{0:T(512)} %copy-done.47) | copy-start | bytes 6148
  1415.7 4.1 copy-start.32
  1415.7 5.3 copy-start.25
  1418.7 4.0 copy-start.22
  (32 other events, 71.1 us)
Sparse Core Ops, SparseCore 0:
  12.3 49.0 all-gather.3
  169.4 99.0 reduce-scatter.4
  270.1 80.0 all-gather.5
  419.6 98.5 reduce-scatter.8
  523.9 46.3 all-gather.7
  874.5 58.3 reduce-scatter.10
  936.2 59.0 reduce-scatter.6
  1002.1 413.5 all-reduce.3
